TPU v7x, 128 devices: a whole 4x4x4 slice. The times are simulated.
128 devices in a mesh: tok: 16 (over x_hi, z, core), wid: 8 (over y, x_lo).
Axes of the slice: x: 4 (x_hi: 2, x_lo: 2; x = x_hi * 2 + x_lo), y: 4, z: 4, core: 2. Of those that a mesh axis runs over, the one named last changes fastest.
Arguments:
- tokens: bfloat16 [9344, 1024], P('tok', 'wid'), may hold values from -6 to 6
- image_ids: int32 [9344], P('tok'), may hold values from 1 to 9360, as said below
- norm_gains: float32 [2, 2, 1024], P(None, None, 'wid'), may hold values from 0.5 to 1.5
- norm_shifts: float32 [2, 2, 1024], P(None, None, 'wid'), may hold values from -1.8 to 1.8
- qkv_weight: bfloat16 [2, 1024, 3, 1024], P(None, 'tok', None, 'wid'), may hold values from -0.1875 to 0.1875
- qv_bias: float32 [2, 2, 1024], P(None, None, 'wid'), may hold values from -3 to 3
- out_weight: bfloat16 [2, 1024, 1024], P(None, 'wid', 'tok'), may hold values from -0.75 to 0.75
- out_bias: float32 [2, 1024], P(None, 'wid'), may hold values from -3 to 3
- up_weight: bfloat16 [2, 1024, 4096], P(None, 'tok', 'wid'), may hold values from -0.1875 to 0.1875
- up_bias: float32 [2, 4096], P(None, 'wid'), may hold values from -3 to 3
- down_weight: bfloat16 [2, 4096, 1024], P(None, 'wid', 'tok'), may hold values from -0.125 to 0.125
- down_bias: float32 [2, 1024], P(None, 'wid'), may hold values from -3 to 3
- out_grad: bfloat16 [9344, 1024], P('tok', 'wid'), may hold values from -6 to 6
Outputs:
- activations: bfloat16 [9344, 1024], P('tok', 'wid')
- input_grad: float32 [9344, 1024], P('tok', 'wid')
- gain_grad: float32 [2, 2, 1024], P(None, None, 'wid')
- shift_grad: float32 [2, 2, 1024], P(None, None, 'wid')
- qkv_grad: float32 [2, 1024, 3, 1024], P(None, 'tok', None, 'wid')
- qv_bias_grad: float32 [2, 2, 1024], P(None, None, 'wid')
- out_weight_grad: float32 [2, 1024, 1024], P(None, 'wid', 'tok')
- out_bias_grad: float32 [2, 1024], P(None, 'wid')
- up_weight_grad: float32 [2, 1024, 4096], P(None, 'tok', 'wid')
- up_bias_grad: float32 [2, 4096], P(None, 'wid')
- down_weight_grad: float32 [2, 4096, 1024], P(None, 'wid', 'tok')
- down_bias_grad: float32 [2, 1024], P(None, 'wid')
Inputs may be any that keep to these rules, and one draw needn't show every extreme that they name: `image_ids`: images 1 to 16, in order, each hold exactly 577 consecutive tokens; each aligned block of 584 tokens holds one whole image; every other token has a number of its own above 16, and the last token of each block is such a token.
All inputs are finite; a program needn't handle non-finite values.
Results may differ from a plain program's by a relative error of at most 0.02.
Values may be sent and summed in bfloat16 or wider, within the bound.
No kernel may reach another device: no remote copies, remote signals or barrier semaphores. Data moves between devices by JAX's collectives and lax.ppermute only.
A program may use at most 128 MiB of HBM per device.

v0:
```python
import jax
import jax.numpy as jnp
from jax import lax
from jax.sharding import PartitionSpec as P

HEAD = 64
LAYERS = 2
EPSILON = 1e-06


def copy_for_each(value, axis):
    copies = jnp.broadcast_to(value, (lax.axis_size(axis), *value.shape))
    return lax.all_to_all(copies, axis, split_axis=0, concat_axis=0, tiled=True)


def over_copies(value, axis):
    everything = copy_for_each(value, axis)
    return jnp.sum(everything, axis=0)


def in_one(arrays, axis):
    line, at, finished = (jnp.concatenate([a.reshape(-1) for a in arrays]), 0, [])
    so_far = over_copies(line, axis)
    for a in arrays:
        finished.append(so_far[at : at + a.size].reshape(a.shape))
        at += a.size
    return tuple(finished)


def in_order(tiles, dim):
    dims = list(tiles.shape[1:])
    dims[dim] *= tiles.shape[0]
    return jnp.moveaxis(tiles, 0, dim).reshape(dims)


def collect(value, axis, dim):
    tiles = copy_for_each(value, axis)
    return in_order(tiles, dim)


def cut_along(value, dim, peers):
    before, after = (value.shape[:dim], value.shape[dim + 1 :])
    return jnp.moveaxis(value.reshape(*before, peers, -1, *after), dim, 0)


def summed_on_arrival(value, axis, dim):
    tiles = cut_along(value, dim, lax.axis_size(axis))
    arrived = lax.all_to_all(tiles, axis, split_axis=0, concat_axis=0, tiled=True)
    return arrived.astype(jnp.float32).sum(axis=0)


def turned_gather(arrays, axis, dims):
    turned = [jnp.moveaxis(a, dim, 0) for a, dim in zip(arrays, dims)]
    both = jnp.concatenate([t.reshape(len(t), -1) for t in turned], axis=1)
    filled, at, finished = (lax.all_gather(both, axis, axis=0, tiled=True), 0, [])
    for t, dim in zip(turned, dims):
        piece = filled[:, at : at + t[0].size].reshape(-1, *t.shape[1:])
        finished.append(jnp.moveaxis(piece, 0, dim))
        at += t[0].size
    return tuple(finished)


def sum_together(arrays, axis, dims):
    peers = lax.axis_size(axis)
    tiles = [cut_along(a, dim, peers) for a, dim in zip(arrays, dims)]
    lines = jnp.concatenate([b.reshape(peers, -1) for b in tiles], axis=1)
    span = max(16, -(-lines.shape[1] // 1024) * 8)
    lines = jnp.pad(lines, ((0, 0), (0, span * 128 - lines.shape[1]))).reshape(-1, 128)
    line, at, finished = (lax.psum_scatter(lines, axis, tiled=True).reshape(-1), 0, [])
    for b in tiles:
        part = b[0]
        finished.append(line[at : at + part.size].reshape(part.shape))
        at += part.size
    return tuple(finished)


def contract_rows(left, right):
    return lax.dot_general(
        left, right, (((0,), (0,)), ((), ())), preferred_element_type=jnp.float32
    )


def contract_cols(left, right):
    return lax.dot_general(
        left, right, (((1,), (1,)), ((), ())), preferred_element_type=jnp.float32
    )


def norm_forward(values, gain, shift, width):
    totals = in_one((jnp.sum(values, axis=1), jnp.sum(values * values, axis=1)), "wid")
    mean = totals[0] / width
    spread = totals[1] / width - mean * mean
    row_scale = lax.rsqrt(spread + EPSILON)
    centred = (values - mean[:, None]) * row_scale[:, None]
    return (centred, row_scale, centred * gain + shift)


def norm_backward(dnormed, centred, row_scale, gain, width):
    scaled = dnormed * gain
    totals = in_one((jnp.sum(scaled, axis=1), jnp.sum(scaled * centred, axis=1)), "wid")
    dvalues = row_scale[:, None] * (
        scaled - totals[0][:, None] / width - centred * (totals[1][:, None] / width)
    )
    return (dvalues, jnp.sum(dnormed * centred, axis=0), jnp.sum(dnormed, axis=0))


def full_rows(values):
    return collect(values, "wid", 1)


def width_sum(partial_value):
    return summed_on_arrival(partial_value.astype(jnp.bfloat16), "wid", 1)


def split_heads(values, heads):
    return values.reshape(values.shape[0], heads, values.shape[1] // heads)


def scores_of(query, keys, token_ids, heads):
    raw = jnp.einsum(
        "qhe,khe->hqk",
        split_heads(query, heads),
        split_heads(keys, heads),
        preferred_element_type=jnp.float32,
    )
    allowed = token_ids[:, None] == token_ids[None, :]
    return jnp.where(allowed[None], raw * HEAD ** (-0.5), -1e30)


def attend(query, keys, values, token_ids, heads):
    scores = scores_of(query, keys, token_ids, heads)
    top = jnp.max(scores, axis=2, keepdims=True)
    expo = jnp.exp(scores - top)
    total = jnp.sum(expo, axis=2, keepdims=True)
    probs = (expo / total).astype(jnp.bfloat16)
    mixed = jnp.einsum(
        "hqk,khe->qhe", probs, split_heads(values, heads), preferred_element_type=jnp.float32
    )
    return (mixed.reshape(query.shape[0], query.shape[1]), top + jnp.log(total))


def attend_back(dmixed, query, keys, values, token_ids, logsum, heads):
    scores = scores_of(query, keys, token_ids, heads)
    probs = jnp.exp(scores - logsum)
    dmix3 = split_heads(dmixed, heads)
    dvalues = jnp.einsum(
        "hqk,qhe->khe", probs.astype(jnp.bfloat16), dmix3, preferred_element_type=jnp.float32
    )
    dprobs = jnp.einsum(
        "qhe,khe->hqk", dmix3, split_heads(values, heads), preferred_element_type=jnp.float32
    )
    centre = jnp.sum(probs * dprobs, axis=2, keepdims=True)
    dscores = (probs * (dprobs - centre)).astype(jnp.bfloat16)
    scale = HEAD ** (-0.5)
    dquery = (
        jnp.einsum(
            "hqk,khe->qhe", dscores, split_heads(keys, heads), preferred_element_type=jnp.float32
        )
        * scale
    )
    dkeys = (
        jnp.einsum(
            "hqk,qhe->khe", dscores, split_heads(query, heads), preferred_element_type=jnp.float32
        )
        * scale
    )
    rows = query.shape[0]
    return (dquery.reshape(rows, -1), dkeys.reshape(rows, -1), dvalues.reshape(rows, -1))


def gelu_slope(pre):
    return (
        0.5 * (1.0 + lax.erf(pre * 0.7071067811865476))
        + pre * jnp.exp(-0.5 * pre * pre) * 0.3989422804014327
    )


def shards(
    tokens,
    image_ids,
    norm_gains,
    norm_shifts,
    qkv_weight,
    qv_bias,
    out_weight,
    out_bias,
    up_weight,
    up_bias,
    down_weight,
    down_bias,
    out_grad,
):
    rows = tokens.shape[0]
    cols = tokens.shape[1]
    width = cols * lax.axis_size("wid")
    heads = cols // HEAD
    state = tokens.astype(jnp.float32)
    kept = []
    saved = []
    for layer in range(LAYERS):
        matrices = turned_gather(
            (qkv_weight[layer], out_weight[layer], up_weight[layer], down_weight[layer]),
            "tok",
            (0, 1, 0, 1),
        )
        qkv_full, out_full, up_full, down_full = matrices
        kept.append(matrices)
        centred1, scale1, normed1 = norm_forward(
            state, norm_gains[layer, 0], norm_shifts[layer, 0], width
        )
        rows1 = full_rows(normed1.astype(jnp.bfloat16))
        proj = jnp.dot(
            rows1, qkv_full.reshape(width, 3 * cols), preferred_element_type=jnp.float32
        ).reshape(rows, 3, cols)
        query = (proj[:, 0] + qv_bias[layer, 0]).astype(jnp.bfloat16)
        keys = proj[:, 1].astype(jnp.bfloat16)
        values = (proj[:, 2] + qv_bias[layer, 1]).astype(jnp.bfloat16)
        mixed, logsum = attend(query, keys, values, image_ids, heads)
        attended = mixed.astype(jnp.bfloat16)
        branch = width_sum(jnp.dot(attended, out_full, preferred_element_type=jnp.float32))
        middle = state + branch + out_bias[layer]
        centred2, scale2, normed2 = norm_forward(
            middle, norm_gains[layer, 1], norm_shifts[layer, 1], width
        )
        rows2 = full_rows(normed2.astype(jnp.bfloat16))
        pre = jnp.dot(rows2, up_full, preferred_element_type=jnp.float32) + up_bias[layer]
        hidden = jax.nn.gelu(pre, approximate=False).astype(jnp.bfloat16)
        state = (
            middle
            + width_sum(jnp.dot(hidden, down_full, preferred_element_type=jnp.float32))
            + down_bias[layer]
        )
        saved.append(
            (
                centred1,
                scale1,
                rows1,
                query,
                keys,
                values,
                logsum,
                attended,
                centred2,
                scale2,
                rows2,
                pre,
                hidden,
            )
        )
    activations = state.astype(jnp.bfloat16)
    grad_state = out_grad.astype(jnp.float32)
    results = []
    for layer in reversed(range(LAYERS)):
        matrices = turned_gather(
            (qkv_weight[layer], out_weight[layer], up_weight[layer], down_weight[layer]),
            "tok",
            (0, 1, 0, 1),
        )
        qkv_full, out_full, up_full, down_full = matrices
        (
            centred1,
            scale1,
            rows1,
            query,
            keys,
            values,
            logsum,
            attended,
            centred2,
            scale2,
            rows2,
            pre,
            hidden,
        ) = saved[layer]
        grad_branch = grad_state.astype(jnp.bfloat16)
        grad_rows = full_rows(grad_branch)
        dhidden = contract_cols(grad_rows, down_full)
        ddown = contract_rows(hidden, grad_rows)
        dpre = (dhidden * gelu_slope(pre)).astype(jnp.bfloat16)
        dup = contract_rows(rows2, dpre)
        dnormed2 = width_sum(contract_cols(dpre, up_full))
        dmiddle, dgain2, dshift2 = norm_backward(
            dnormed2, centred2, scale2, norm_gains[layer, 1], width
        )
        grad_middle = grad_state + dmiddle
        grad_attn = grad_middle.astype(jnp.bfloat16)
        attn_rows = full_rows(grad_attn)
        dmixed = contract_cols(attn_rows, out_full).astype(jnp.bfloat16)
        dout = contract_rows(attended, attn_rows)
        dquery, dkeys, dvalues = attend_back(dmixed, query, keys, values, image_ids, logsum, heads)
        dquery = dquery.astype(jnp.bfloat16)
        dkeys = dkeys.astype(jnp.bfloat16)
        dvalues = dvalues.astype(jnp.bfloat16)
        dproj = jnp.stack([dquery, dkeys, dvalues], axis=1).reshape(rows, 3 * cols)
        dqkv = contract_rows(rows1, dproj).reshape(width, 3, cols)
        dnormed1 = width_sum(contract_cols(dproj, qkv_full.reshape(width, 3 * cols)))
        dinput, dgain1, dshift1 = norm_backward(
            dnormed1, centred1, scale1, norm_gains[layer, 0], width
        )
        grad_state = grad_middle + dinput
        weight_parts = tuple(
            (
                part.astype(jnp.float32)
                for part in sum_together(
                    (
                        dqkv.astype(jnp.bfloat16),
                        dout.astype(jnp.bfloat16),
                        dup.astype(jnp.bfloat16),
                        ddown.astype(jnp.bfloat16),
                    ),
                    "tok",
                    (0, 1, 0, 1),
                )
            )
        )
        vector_parts = in_one(
            (
                jnp.stack([dgain1, dgain2]),
                jnp.stack([dshift1, dshift2]),
                jnp.stack(
                    [
                        jnp.sum(dquery, axis=0, dtype=jnp.float32),
                        jnp.sum(dvalues, axis=0, dtype=jnp.float32),
                    ]
                ),
                jnp.sum(grad_attn, axis=0, dtype=jnp.float32),
                jnp.sum(dpre, axis=0, dtype=jnp.float32),
                jnp.sum(grad_branch, axis=0, dtype=jnp.float32),
            ),
            "tok",
        )
        results.append((weight_parts, vector_parts))
    results = results[::-1]
    gain_grad = jnp.stack([item[1][0] for item in results])
    shift_grad = jnp.stack([item[1][1] for item in results])
    qkv_grad = jnp.stack([item[0][0] for item in results])
    qv_bias_grad = jnp.stack([item[1][2] for item in results])
    out_weight_grad = jnp.stack([item[0][1] for item in results])
    out_bias_grad = jnp.stack([item[1][3] for item in results])
    up_weight_grad = jnp.stack([item[0][2] for item in results])
    up_bias_grad = jnp.stack([item[1][4] for item in results])
    down_weight_grad = jnp.stack([item[0][3] for item in results])
    down_bias_grad = jnp.stack([item[1][5] for item in results])
    return (
        activations,
        grad_state,
        gain_grad,
        shift_grad,
        qkv_grad,
        qv_bias_grad,
        out_weight_grad,
        out_bias_grad,
        up_weight_grad,
        up_bias_grad,
        down_weight_grad,
        down_bias_grad,
    )


def solution(mesh):
    placed = (
        P("tok", "wid"),
        P("tok"),
        P(None, None, "wid"),
        P(None, None, "wid"),
        P(None, "tok", None, "wid"),
        P(None, None, "wid"),
        P(None, "wid", "tok"),
        P(None, "wid"),
        P(None, "tok", "wid"),
        P(None, "wid"),
        P(None, "wid", "tok"),
        P(None, "wid"),
        P("tok", "wid"),
    )
    return jax.shard_map(
        shards,
        mesh=mesh,
        in_specs=placed,
        out_specs=(
            P("tok", "wid"),
            P("tok", "wid"),
            P(None, None, "wid"),
            P(None, None, "wid"),
            P(None, "tok", None, "wid"),
            P(None, None, "wid"),
            P(None, "wid", "tok"),
            P(None, "wid"),
            P(None, "tok", "wid"),
            P(None, "wid"),
            P(None, "wid", "tok"),
            P(None, "wid"),
        ),
        check_vma=False,
    )
```

profile of v0, /device:TPU:0, one launch (start us, length us, event | category | flops | bytes accessed | tf_op | source)
XLA Modules:
  0.0 663.1 jit_solution(15200785847453675437)
XLA Ops:
  12.4 5.5 all-to-all-start
  18.4 5.7 all-to-all-done
  25.7 3.7 all-to-all-start.1
  31.2 14.3 %all-to-all-done.1 = bf16[8,584,128]{2,1,0:T(8,128)(2,1)S(1)} async-done(((bf16[8,584,128]{2,1,0:T(8,128)(2,1)}), bf16[8,584,128]{2,1,0:T(8,128)(2,1)S(1)}, u32[]{:S(2)}, u32[]{:S(2)}) %all-to-all-start.1) | async-done | bytes 1196064 | tf_op jit(solution)/shard_map/all_to_all | solution.py:13
  47.1 17.8 %all-gather.3.cloned.1.call-done = bf16[1024,1536]{1,0:T(8,128)(2,1)} async-done(((bf16[64,1536]{1,0:T(8,128)(2,1)}), bf16[1024,1536]{1,0:T(8,128)(2,1)}) %all-gather.3.cloned.1.call-update) | async-done | bytes 3145744 | tf_op jit(solution)/shard_map/all_gather | solution.py:55
  75.7 4.4 all-to-all-start.2
  81.5 16.7 %all-to-all-done.2 = bf16[8,584,128]{2,1,0:T(8,128)(2,1)} async-done(((bf16[8,584,128]{2,1,0:T(8,128)(2,1)}), bf16[8,584,128]{2,1,0:T(8,128)(2,1)}, u32[]{:S(2)}, u32[]{:S(2)}) %all-to-all-start.2) | async-done | bytes 1196064 | tf_op jit(solution)/shard_map/all_to_all | solution.py:48
  100.0 8.8 %all_to_all.140 = f32[8,1,1168]{2,1,0:T(1,128)S(1)} all-to-all(f32[8,1,1168]{2,1,0:T(1,128)S(1)} %broadcast_in_dim.120), channel_id=1, replica_groups=mesh['tok'=16,'wid'=8] {'wid'}, dimensions={0} | all-to-all | bytes 74752 | tf_op jit(solution)/shard_map/all_to_all | solution.py:13
  110.4 4.4 all-to-all-start.4
  115.3 24.1 %all-to-all-done.4 = bf16[8,584,128]{2,1,0:T(8,128)(2,1)} async-done(((bf16[8,584,128]{2,1,0:T(8,128)(2,1)}), bf16[8,584,128]{2,1,0:T(8,128)(2,1)}, u32[]{:S(2)}, u32[]{:S(2)}) %all-to-all-start.4) | async-done | bytes 1196064 | tf_op jit(solution)/shard_map/all_to_all | solution.py:13
  139.5 5.8 fusion.25
  148.8 4.6 all-to-all-start.5
  153.9 15.8 %all-to-all-done.5 = bf16[8,584,128]{2,1,0:T(8,128)(2,1)} async-done(((bf16[8,584,128]{2,1,0:T(8,128)(2,1)}), bf16[8,584,128]{2,1,0:T(8,128)(2,1)}, u32[]{:S(2)}, u32[]{:S(2)}) %all-to-all-start.5) | async-done | bytes 1196064 | tf_op jit(solution)/shard_map/all_to_all | solution.py:48
  172.1 8.8 %all_to_all.141 = f32[8,1,1168]{2,1,0:T(1,128)S(1)} all-to-all(f32[8,1,1168]{2,1,0:T(1,128)S(1)} %broadcast_in_dim.122), channel_id=1, replica_groups=mesh['tok'=16,'wid'=8] {'wid'}, dimensions={0} | all-to-all | bytes 74752 | tf_op jit(solution)/shard_map/all_to_all | solution.py:13
  183.4 4.4 all-to-all-start.7
  192.5 10.9 %all-to-all-done.7 = bf16[8,584,128]{2,1,0:T(8,128)(2,1)} async-done(((bf16[8,584,128]{2,1,0:T(8,128)(2,1)}), bf16[8,584,128]{2,1,0:T(8,128)(2,1)}, u32[]{:S(2)}, u32[]{:S(2)}) %all-to-all-start.7) | async-done | bytes 1196064 | tf_op jit(solution)/shard_map/all_to_all | solution.py:13
  205.9 3.1 reshape.602
  225.0 17.7 %all_to_all.142 = bf16[8,584,128]{2,1,0:T(8,128)(2,1)S(1)} all-to-all(bf16[8,584,128]{2,1,0:T(8,128)(2,1)S(1)} %bitcast.374), channel_id=1, replica_groups=mesh['tok'=16,'wid'=8] {'wid'}, dimensions={0} | all-to-all | bytes 2392064 | tf_op jit(solution)/shard_map/all_to_all | solution.py:48
  244.7 8.7 %all_to_all.143 = f32[8,1,1168]{2,1,0:T(1,128)S(1)} all-to-all(f32[8,1,1168]{2,1,0:T(1,128)S(1)} %broadcast_in_dim.124), channel_id=1, replica_groups=mesh['tok'=16,'wid'=8] {'wid'}, dimensions={0} | all-to-all | bytes 74752 | tf_op jit(solution)/shard_map/all_to_all | solution.py:13
  254.9 16.3 %all_to_all.144 = bf16[8,584,128]{2,1,0:T(8,128)(2,1)} all-to-all(bf16[8,584,128]{2,1,0:T(8,128)(2,1)S(1)} %broadcast_in_dim.125), channel_id=1, replica_groups=mesh['tok'=16,'wid'=8] {'wid'}, dimensions={0} | all-to-all | bytes 2392064 | tf_op jit(solution)/shard_map/all_to_all | solution.py:13
  272.4 4.6 all-to-all-start.12
  277.0 6.0 fusion.28
  283.0 6.8 %all-to-all-done.12 = bf16[8,584,128]{2,1,0:T(8,128)(2,1)} async-done(((bf16[8,584,128]{2,1,0:T(8,128)(2,1)}), bf16[8,584,128]{2,1,0:T(8,128)(2,1)}, u32[]{:S(2)}, u32[]{:S(2)}) %all-to-all-start.12) | async-done | bytes 1196064 | tf_op jit(solution)/shard_map/all_to_all | solution.py:13
  289.8 3.7 convert_reduce_fusion.12
  297.0 4.3 all-to-all-start.13
  304.8 8.9 %all-to-all-done.13 = bf16[8,584,128]{2,1,0:T(8,128)(2,1)} async-done(((bf16[8,584,128]{2,1,0:T(8,128)(2,1)}), bf16[8,584,128]{2,1,0:T(8,128)(2,1)}, u32[]{:S(2)}, u32[]{:S(2)}) %all-to-all-start.13) | async-done | bytes 1196064 | tf_op jit(solution)/shard_map/all_to_all | solution.py:48
  313.7 4.3 all-to-all-start.11
  321.6 8.9 %all-to-all-done.11 = bf16[8,584,128]{2,1,0:T(8,128)(2,1)} async-done(((bf16[8,584,128]{2,1,0:T(8,128)(2,1)}), bf16[8,584,128]{2,1,0:T(8,128)(2,1)}, u32[]{:S(2)}, u32[]{:S(2)}) %all-to-all-start.11) | async-done | bytes 1196064 | tf_op jit(solution)/shard_map/all_to_all | solution.py:48
  331.2 3.3 all-to-all-start.14
  336.7 4.0 all-to-all-done.14
  340.9 2.9 convert_reduce_fusion.20
  344.9 4.5 all-to-all-start.15
  349.5 12.3 %all-to-all-done.15 = bf16[8,584,128]{2,1,0:T(8,128)(2,1)} async-done(((bf16[8,584,128]{2,1,0:T(8,128)(2,1)}), bf16[8,584,128]{2,1,0:T(8,128)(2,1)}, u32[]{:S(2)}, u32[]{:S(2)}) %all-to-all-start.15) | async-done | bytes 1196064 | tf_op jit(solution)/shard_map/all_to_all | solution.py:13
  366.0 3.3 convert_reduce_fusion.16
  376.4 15.1 %all_to_all.145 = bf16[8,584,128]{2,1,0:T(8,128)(2,1)S(1)} all-to-all(bf16[8,584,128]{2,1,0:T(8,128)(2,1)S(1)} %bitcast.375), channel_id=1, replica_groups=mesh['tok'=16,'wid'=8] {'wid'}, dimensions={0} | all-to-all | bytes 2392064 | tf_op jit(solution)/shard_map/all_to_all | solution.py:48
  393.2 8.8 %all_to_all.146 = f32[8,1,1168]{2,1,0:T(1,128)S(1)} all-to-all(f32[8,1,1168]{2,1,0:T(1,128)S(1)} %broadcast_in_dim.129), channel_id=1, replica_groups=mesh['tok'=16,'wid'=8] {'wid'}, dimensions={0} | all-to-all | bytes 74752 | tf_op jit(solution)/shard_map/all_to_all | solution.py:13
  406.0 4.2 all-to-all-start.18
  410.3 12.3 %all-to-all-done.18 = bf16[8,584,128]{2,1,0:T(8,128)(2,1)} async-done(((bf16[8,584,128]{2,1,0:T(8,128)(2,1)}), bf16[8,584,128]{2,1,0:T(8,128)(2,1)}, u32[]{:S(2)}, u32[]{:S(2)}) %all-to-all-start.18) | async-done | bytes 1196064 | tf_op jit(solution)/shard_map/all_to_all | solution.py:13
  422.6 3.1 convert_reduce_fusion.13
  429.2 4.7 all-to-all-start.19
  434.0 3.4 convolution_convert_fusion.9
  439.8 3.5 convolution_convert_fusion.8
  448.3 3.7 reshape.599
  452.0 3.3 convolution_convert_fusion.12
  459.2 5.7 all-to-all-start.20
  473.3 2.8 copy.241
  482.7 5.8 all-to-all-start.21
  488.6 3.1 pad_maximum_fusion.1
  491.9 4.0 reshape.600
  496.2 3.4 convolution_convert_fusion.11
  502.0 3.5 convolution_convert_fusion.10
  507.8 2.8 copy.239
  510.6 3.7 reshape.594
  529.7 2.8 pad_maximum_fusion
  532.4 4.1 reshape.595
  538.0 3.7 all-to-all-start.25
  545.0 4.5 all-to-all-done.25
  549.5 5.6 all-to-all-start.22
  555.4 16.9 %reduce-scatter.5.cloned.1.call-done = bf16[768,128]{1,0:T(8,128)(2,1)} async-done(((bf16[12288,128]{1,0:T(8,128)(2,1)}), bf16[768,128]{1,0:T(8,128)(2,1)}) %reduce-scatter.5.cloned.1.call-update) | async-done | bytes 196624 | tf_op jit(solution)/shard_map/reduce_scatter | solution.py:69
  577.1 4.3 all-to-all-start.23
  581.5 6.2 all-to-all-done.23
  588.4 5.2 all-to-all-start.24
  594.8 6.6 all-to-all-done.24
  605.0 45.5 %reduce-scatter.3.cloned.1.call-done = bf16[768,128]{1,0:T(8,128)(2,1)} async-done(((bf16[12288,128]{1,0:T(8,128)(2,1)}), bf16[768,128]{1,0:T(8,128)(2,1)}) %reduce-scatter.3.cloned.1.call-update) | async-done | bytes 196624 | tf_op jit(solution)/shard_map/reduce_scatter | solution.py:69
  (372 shorter events, 166.3 us)
Async XLA Ops:
  7.2 4.2 copy-start.6
  7.2 10.6 %copy-start.53 = (f32[2,2,128]{2,1,0:T(2,128)S(1)}, f32[2,2,128]{2,1,0:T(2,128)}, u32[]{:S(2)}) copy-start(f32[2,2,128]{2,1,0:T(2,128)} %param.16) | copy-start | bytes 6148
  7.2 10.6 %copy-start.54 = (f32[2,2,128]{2,1,0:T(2,128)S(1)}, f32[2,2,128]{2,1,0:T(2,128)}, u32[]{:S(2)}) copy-start(f32[2,2,128]{2,1,0:T(2,128)} %param.15) | copy-start | bytes 6148
  7.2 57.7 %all-gather.3.cloned.1.call-start = ((), (), s32[]{:S(2)}) async-start(), calls=%async_computation.28 | async-start | bytes 3342336 | tf_op jit(solution)/shard_map/all_gather | solution.py:55
  12.4 11.8 %all-to-all-start = ((f32[8,1,1168]{2,1,0:T(1,128)}), f32[8,1,1168]{2,1,0:T(1,128)S(1)}, u32[]{:S(2)}, u32[]{:S(2)}) async-start(f32[8,1,1168]{2,1,0:T(1,128)} %broadcast_in_dim.60), calls=%async_computation | async-start | bytes 81920 | tf_op jit(solution)/shard_map/all_to_all | solution.py:13
  18.4 6.1 copy-start.37
  18.4 90.5 %copy-start.39 = (f32[128]{0:T(128)}, f32[128]{0:T(128)S(1)}, u32[]{:S(2)}) copy-start(f32[128]{0:T(128)S(1)} %get-tuple-element.188) | copy-start | bytes 1540
  18.4 162.6 %copy-start.41 = (f32[128]{0:T(128)}, f32[128]{0:T(128)S(1)}, u32[]{:S(2)}) copy-start(f32[128]{0:T(128)S(1)} %get-tuple-element.186) | copy-start | bytes 1540
  25.7 3.7 copy-start.51
  25.7 4.4 copy-start.35
  25.7 19.8 %all-to-all-start.1 = ((bf16[8,584,128]{2,1,0:T(8,128)(2,1)}), bf16[8,584,128]{2,1,0:T(8,128)(2,1)S(1)}, u32[]{:S(2)}, u32[]{:S(2)}) async-start(bf16[8,584,128]{2,1,0:T(8,128)(2,1)} %broadcast_in_dim.61), calls=%async_computation.1 | async-start | bytes 2392064 | tf_op jit(solution)/shard_map/all_to_all | solution.py:13
  30.0 39.3 %copy-start.44 = (f32[2,64]{1,0:T(2,128)}, f32[2,64]{1,0:T(2,128)S(1)}, u32[]{:S(2)}) copy-start(f32[2,64]{1,0:T(2,128)S(1)} %add.219) | copy-start | bytes 1540
  30.1 41.6 %copy-start.56 = (f32[2,64]{1,0:T(2,128)}, f32[2,64]{1,0:T(2,128)S(1)}, u32[]{:S(2)}) copy-start(f32[2,64]{1,0:T(2,128)S(1)} %add.216) | copy-start | bytes 1540
  47.1 19.3 %copy-start.19 = (bf16[584,1024,1]{1,0,2:T(8,128)(2,1)S(1)}, bf16[584,1024,1]{1,0,2:T(8,128)(2,1)}, u32[]{:S(2)}) copy-start(bf16[584,1024,1]{1,0,2:T(8,128)(2,1)} %reshape.601) | copy-start | bytes 3588100
  67.5 3.8 copy-start.13
  72.9 2.8 copy-start.32
  75.7 5.3 copy-start.62
  75.7 22.4 %all-to-all-start.2 = ((bf16[8,584,128]{2,1,0:T(8,128)(2,1)}), bf16[8,584,128]{2,1,0:T(8,128)(2,1)}, u32[]{:S(2)}, u32[]{:S(2)}) async-start(bf16[8,584,128]{2,1,0:T(8,128)(2,1)} %bitcast.368), calls=%async_computation.2 | async-start | bytes 2392064 | tf_op jit(solution)/shard_map/all_to_all | solution.py:48
  80.2 107.8 %all-gather.5.cloned.1.call-start = ((), (), s32[]{:S(2)}) async-start(), calls=%async_computation.29 | async-start | bytes 3342336 | tf_op jit(solution)/shard_map/all_gather | solution.py:55
  110.4 4.4 copy-start.43
  110.4 29.1 %all-to-all-start.4 = ((bf16[8,584,128]{2,1,0:T(8,128)(2,1)}), bf16[8,584,128]{2,1,0:T(8,128)(2,1)}, u32[]{:S(2)}, u32[]{:S(2)}) async-start(bf16[8,584,128]{2,1,0:T(8,128)(2,1)} %broadcast_in_dim.121), calls=%async_computation.4 | async-start | bytes 2392064 | tf_op jit(solution)/shard_map/all_to_all | solution.py:13
  148.8 4.6 copy-start.63
  148.8 20.9 %all-to-all-start.5 = ((bf16[8,584,128]{2,1,0:T(8,128)(2,1)}), bf16[8,584,128]{2,1,0:T(8,128)(2,1)}, u32[]{:S(2)}, u32[]{:S(2)}) async-start(bf16[8,584,128]{2,1,0:T(8,128)(2,1)} %bitcast.373), calls=%async_computation.5 | async-start | bytes 2392064 | tf_op jit(solution)/shard_map/all_to_all | solution.py:48
  183.4 4.4 copy-start.69
  183.4 4.5 copy-start.68
  183.4 20.0 %all-to-all-start.7 = ((bf16[8,584,128]{2,1,0:T(8,128)(2,1)}), bf16[8,584,128]{2,1,0:T(8,128)(2,1)}, u32[]{:S(2)}, u32[]{:S(2)}) async-start(bf16[8,584,128]{2,1,0:T(8,128)(2,1)} %broadcast_in_dim.123), calls=%async_computation.7 | async-start | bytes 2392064 | tf_op jit(solution)/shard_map/all_to_all | solution.py:13
  187.9 32.8 %copy-start.58 = (f32[2,64]{1,0:T(2,128)}, f32[2,64]{1,0:T(2,128)S(1)}, u32[]{:S(2)}) copy-start(f32[2,64]{1,0:T(2,128)S(1)} %add.241) | copy-start | bytes 1540
  188.0 30.2 %copy-start.46 = (f32[2,64]{1,0:T(2,128)}, f32[2,64]{1,0:T(2,128)S(1)}, u32[]{:S(2)}) copy-start(f32[2,64]{1,0:T(2,128)S(1)} %add.244) | copy-start | bytes 1540
  254.9 16.3 %copy-start.31 = (bf16[584,128]{1,0:T(8,128)(2,1)S(1)}, bf16[584,128]{1,0:T(8,128)(2,1)}, u32[]{:S(2)}) copy-start(bf16[584,128]{1,0:T(8,128)(2,1)} %param.25) | copy-start | bytes 448516
  272.4 4.6 copy-start.55
  272.4 17.4 %all-to-all-start.12 = ((bf16[8,584,128]{2,1,0:T(8,128)(2,1)}), bf16[8,584,128]{2,1,0:T(8,128)(2,1)}, u32[]{:S(2)}, u32[]{:S(2)}) async-start(bf16[8,584,128]{2,1,0:T(8,128)(2,1)} %broadcast_in_dim.126), calls=%async_computation.12 | async-start | bytes 2392064 | tf_op jit(solution)/shard_map/all_to_all | solution.py:13
  297.0 16.6 %all-to-all-start.13 = ((bf16[8,584,128]{2,1,0:T(8,128)(2,1)}), bf16[8,584,128]{2,1,0:T(8,128)(2,1)}, u32[]{:S(2)}, u32[]{:S(2)}) async-start(bf16[8,584,128]{2,1,0:T(8,128)(2,1)} %bitcast.372), calls=%async_computation.13 | async-start | bytes 2392064 | tf_op jit(solution)/shard_map/all_to_all | solution.py:48
  313.7 16.9 %all-to-all-start.11 = ((bf16[8,584,128]{2,1,0:T(8,128)(2,1)}), bf16[8,584,128]{2,1,0:T(8,128)(2,1)}, u32[]{:S(2)}, u32[]{:S(2)}) async-start(bf16[8,584,128]{2,1,0:T(8,128)(2,1)} %bitcast.370), calls=%async_computation.11 | async-start | bytes 2392064 | tf_op jit(solution)/shard_map/all_to_all | solution.py:48
  317.9 2.7 copy-start.4
  317.9 2.7 copy-start.36
  331.2 9.6 %all-to-all-start.14 = ((f32[8,1,1168]{2,1,0:T(1,128)}), f32[8,1,1168]{2,1,0:T(1,128)S(1)}, u32[]{:S(2)}, u32[]{:S(2)}) async-start(f32[8,1,1168]{2,1,0:T(1,128)} %broadcast_in_dim.127), calls=%async_computation.14 | async-start | bytes 81920 | tf_op jit(solution)/shard_map/all_to_all | solution.py:13
  344.9 16.8 %all-to-all-start.15 = ((bf16[8,584,128]{2,1,0:T(8,128)(2,1)}), bf16[8,584,128]{2,1,0:T(8,128)(2,1)}, u32[]{:S(2)}, u32[]{:S(2)}) async-start(bf16[8,584,128]{2,1,0:T(8,128)(2,1)} %broadcast_in_dim.128), calls=%async_computation.15 | async-start | bytes 2392064 | tf_op jit(solution)/shard_map/all_to_all | solution.py:13
  366.0 3.3 copy-start.1
  366.0 3.3 copy-start.12
  366.0 3.3 copy-start.59
  369.3 4.8 copy-start.23
  406.0 16.6 %all-to-all-start.18 = ((bf16[8,584,128]{2,1,0:T(8,128)(2,1)}), bf16[8,584,128]{2,1,0:T(8,128)(2,1)}, u32[]{:S(2)}, u32[]{:S(2)}) async-start(bf16[8,584,128]{2,1,0:T(8,128)(2,1)} %broadcast_in_dim.130), calls=%async_computation.18 | async-start | bytes 2392064 | tf_op jit(solution)/shard_map/all_to_all | solution.py:13
  425.7 2.3 copy-start.72
  429.2 26.0 %all-to-all-start.19 = ((bf16[8,584,128]{2,1,0:T(8,128)(2,1)}), bf16[8,584,128]{2,1,0:T(8,128)(2,1)}, u32[]{:S(2)}, u32[]{:S(2)}) async-start(bf16[8,584,128]{2,1,0:T(8,128)(2,1)} %bitcast.369), calls=%async_computation.19 | async-start | bytes 2392064 | tf_op jit(solution)/shard_map/all_to_all | solution.py:48
  455.2 2.8 copy-start.40
  459.2 19.4 %all-to-all-start.20 = ((f32[8,1,1168]{2,1,0:T(1,128)}), f32[8,1,1168]{2,1,0:T(1,128)S(1)}, u32[]{:S(2)}, u32[]{:S(2)}) async-start(f32[8,1,1168]{2,1,0:T(1,128)} %broadcast_in_dim.131), calls=%async_computation.20 | async-start | bytes 81920 | tf_op jit(solution)/shard_map/all_to_all | solution.py:13
  482.7 5.9 copy-start.22
  482.7 31.6 %all-to-all-start.21 = ((bf16[8,584,128]{2,1,0:T(8,128)(2,1)}), bf16[8,584,128]{2,1,0:T(8,128)(2,1)}, u32[]{:S(2)}, u32[]{:S(2)}) async-start(bf16[8,584,128]{2,1,0:T(8,128)(2,1)} %broadcast_in_dim.132), calls=%async_computation.21 | async-start | bytes 2392064 | tf_op jit(solution)/shard_map/all_to_all | solution.py:13
  488.5 3.2 copy-start.60
  488.5 3.3 copy-start.61
  488.5 83.8 %reduce-scatter.5.cloned.1.call-start = ((), (), s32[]{:S(2)}) async-start(), calls=%async_computation.31 | async-start | bytes 3342336 | tf_op jit(solution)/shard_map/reduce_scatter | solution.py:69
  495.9 154.5 %reduce-scatter.3.cloned.1.call-start = ((), (), s32[]{:S(2)}) async-start(), calls=%async_computation.30 | async-start | bytes 3342336 | tf_op jit(solution)/shard_map/reduce_scatter | solution.py:69
  521.8 3.7 copy-start.27
  536.5 5.1 copy-start.26
  536.5 5.1 copy-start.28
  536.6 5.1 copy-start.30
  538.0 11.5 %all-to-all-start.25 = ((f32[16,1,1536]{2,1,0:T(1,128)}), f32[16,1,1536]{2,1,0:T(1,128)S(1)}, u32[]{:S(2)}, u32[]{:S(2)}) async-start(f32[16,1,1536]{2,1,0:T(1,128)} %broadcast_in_dim.135), calls=%async_computation.25 | async-start | bytes 196608 | tf_op jit(solution)/shard_map/all_to_all | solution.py:13
  549.5 25.6 %all-to-all-start.22 = ((bf16[8,584,128]{2,1,0:T(8,128)(2,1)}), bf16[8,584,128]{2,1,0:T(8,128)(2,1)S(1)}, u32[]{:S(2)}, u32[]{:S(2)}) async-start(bf16[8,584,128]{2,1,0:T(8,128)(2,1)} %bitcast.351), calls=%async_computation.22 | async-start | bytes 2392064 | tf_op jit(solution)/shard_map/all_to_all | solution.py:48
  555.2 20.7 %copy-start.38 = (f32[128]{0:T(128)S(1)}, f32[128]{0:T(128)}, u32[]{:S(2)}) copy-start(f32[128]{0:T(128)} %copy-done.37) | copy-start | bytes 1540
  574.9 6.6 copy-start.67
  574.9 6.6 copy-start.66
  575.1 18.6 %copy-start.21 = (f32[584,128]{1,0:T(8,128)S(1)}, f32[584,128]{1,0:T(8,128)}, u32[]{:S(2)}) copy-start(f32[584,128]{1,0:T(8,128)} %get-tuple-element.97) | copy-start | bytes 897028
  577.1 10.6 %all-to-all-start.23 = ((f32[8,1,1168]{2,1,0:T(1,128)}), f32[8,1,1168]{2,1,0:T(1,128)S(1)}, u32[]{:S(2)}, u32[]{:S(2)}) async-start(f32[8,1,1168]{2,1,0:T(1,128)} %broadcast_in_dim.133), calls=%async_computation.23 | async-start | bytes 81920 | tf_op jit(solution)/shard_map/all_to_all | solution.py:13
  588.4 13.0 %all-to-all-start.24 = ((f32[16,1,1536]{2,1,0:T(1,128)}), f32[16,1,1536]{2,1,0:T(1,128)S(1)}, u32[]{:S(2)}, u32[]{:S(2)}) async-start(f32[16,1,1536]{2,1,0:T(1,128)} %broadcast_in_dim.134), calls=%async_computation.24 | async-start | bytes 196608 | tf_op jit(solution)/shard_map/all_to_all | solution.py:13
  (32 other events, 35.6 us)
Sparse Core Ops, SparseCore 0:
  11.5 53.3 all-gather.2
  84.1 59.2 all-gather.4
  496.1 76.2 reduce-scatter.4
  576.3 74.1 reduce-scatter.2
where the time goes:
time: 676 us; the launch traced here: 663 us
  waiting for transfers between devices  238 us (35%)
  local copies, waits for them, and re-layouts  111 us (16%)
  starting transfers between devices  87.5 us (13%)
  blocking collectives  84.3 us (12%)
  matrix products  81.4 us (12%)
  other arithmetic  45.3 us (7%)
  between operations  15.3 us (2%)
    all_to_all x13, waiting for transfers between devices, copy_for_each(): return lax.all_to_all(copies, axis, split_axis=0, concat_axis=0, tiled=True)  108 us
    reduce_scatter x2, waiting for transfers between devices, sum_together(): lax.psum_scatter(lines, axis, tiled=True).reshape(-1)  62.4 us
    all_to_all x13, starting transfers between devices, copy_for_each(): return lax.all_to_all(copies, axis, split_axis=0, concat_axis=0, tiled=True)  59.3 us
    all_to_all x5, blocking collectives, copy_for_each(): return lax.all_to_all(copies, axis, split_axis=0, concat_axis=0, tiled=True)  51.4 us
    all_to_all x6, waiting for transfers between devices, summed_on_arrival(): lax.all_to_all(tiles, axis, split_axis=0, concat_axis=0, tiled=True)  50.2 us
    all_to_all x2, blocking collectives, summed_on_arrival(): lax.all_to_all(tiles, axis, split_axis=0, concat_axis=0, tiled=True)  32.8 us
    all_to_all x6, starting transfers between devices, summed_on_arrival(): lax.all_to_all(tiles, axis, split_axis=0, concat_axis=0, tiled=True)  27.9 us
    dot_general x8, matrix products, contract_rows(): lax.dot_general(left, right, (((0,), (0,)), ((), ())), preferred_element_...  23.1 us
  transfers between devices with their start and end apart: 23, of which 18 were waited for; matrix products, arithmetic and copies ran while one was open for 21% of the time, Pallas kernels for 0%

commit v1 on v0

--- a/solution.py
+++ b/solution.py
@@ -52,7 +52,13 @@
 def turned_gather(arrays, axis, dims):
     turned = [jnp.moveaxis(a, dim, 0) for a, dim in zip(arrays, dims)]
     both = jnp.concatenate([t.reshape(len(t), -1) for t in turned], axis=1)
-    filled, at, finished = (lax.all_gather(both, axis, axis=0, tiled=True), 0, [])
+    filled, at, finished = (
+        jnp.concatenate(
+            lax.all_to_all(jnp.stack([both] * lax.axis_size(axis)), axis, 0, 0), axis=0
+        ),
+        0,
+        [],
+    )
     for t, dim in zip(turned, dims):
         piece = filled[:, at : at + t[0].size].reshape(-1, *t.shape[1:])
         finished.append(jnp.moveaxis(piece, 0, dim))

time: 676 us -> 770 us (1.14)
  waiting for transfers between devices: 238 us -> 296 us
  starting transfers between devices: 87.5 us -> 117 us
  local copies, waits for them, and re-layouts: 111 us -> 126 us
    all_to_all x0 -> x2, waiting for transfers between devices: none -> 73.7 us  [turned_gather(): lax.all_to_all(jnp.stack([both] * lax.axis_size(axis)), axis, 0, 0)]
    all_to_all x0 -> x2, starting transfers between devices: none -> 18.4 us  [turned_gather(): lax.all_to_all(jnp.stack([both] * lax.axis_size(axis)), axis, 0, 0)]
    all_gather x2 -> x0, waiting for transfers between devices: 17.8 us -> none  [turned_gather(): lax.all_gather(both, axis, axis=0, tiled=True)]
    all_to_all x13 -> x14, starting transfers between devices: 59.3 us -> 70.3 us  [copy_for_each(): return lax.all_to_all(copies, axis, split_axis=0, concat_axis=0, tiled=True)]
    all_to_all x5 -> x4, blocking collectives: 51.4 us -> 45 us  [copy_for_each(): return lax.all_to_all(copies, axis, split_axis=0, concat_axis=0, tiled=True)]
    all_to_all x13 -> x14, waiting for transfers between devices: 108 us -> 106 us  [copy_for_each(): return lax.all_to_all(copies, axis, split_axis=0, concat_axis=0, tiled=True)]
  transfers between devices with their start and end apart: 23 -> 24, of which waited for: 18 -> 20; matrix products, arithmetic and copies ran while one was open for 21% -> 17% of each run, Pallas kernels for 0% -> 0%
where the time goes in v1:
time: 770 us; the launch traced here: 760 us
  waiting for transfers between devices  296 us (38%)
  local copies, waits for them, and re-layouts  126 us (16%)
  starting transfers between devices  117 us (15%)
  matrix products  80.2 us (10%)
  blocking collectives  80.1 us (10%)
  other arithmetic  45.5 us (6%)
  between operations  15.9 us (2%)
    all_to_all x14, waiting for transfers between devices, copy_for_each(): return lax.all_to_all(copies, axis, split_axis=0, concat_axis=0, tiled=True)  106 us
    all_to_all x2, waiting for transfers between devices, turned_gather(): lax.all_to_all(jnp.stack([both] * lax.axis_size(axis)), axis, 0, 0)  73.7 us
    all_to_all x14, starting transfers between devices, copy_for_each(): return lax.all_to_all(copies, axis, split_axis=0, concat_axis=0, tiled=True)  70.3 us
    reduce_scatter x2, waiting for transfers between devices, sum_together(): lax.psum_scatter(lines, axis, tiled=True).reshape(-1)  64.5 us
    all_to_all x6, waiting for transfers between devices, summed_on_arrival(): lax.all_to_all(tiles, axis, split_axis=0, concat_axis=0, tiled=True)  51.8 us
    all_to_all x4, blocking collectives, copy_for_each(): return lax.all_to_all(copies, axis, split_axis=0, concat_axis=0, tiled=True)  45 us
    all_to_all x2, blocking collectives, summed_on_arrival(): lax.all_to_all(tiles, axis, split_axis=0, concat_axis=0, tiled=True)  35.2 us
    all_to_all x6, starting transfers between devices, summed_on_arrival(): lax.all_to_all(tiles, axis, split_axis=0, concat_axis=0, tiled=True)  27.6 us
  transfers between devices with their start and end apart: 24, of which 20 were waited for; matrix products, arithmetic and copies ran while one was open for 17% of the time, Pallas kernels for 0%

profile of v1, /device:TPU:0, one launch (start us, length us, event | category | flops | bytes accessed | tf_op | source)
XLA Modules:
  0.0 759.9 jit_solution(13742780744946851022)
XLA Ops:
  9.0 5.5 all-to-all-start
  15.9 4.9 all-to-all-done
  23.8 3.7 all-to-all-start.1
  30.2 13.5 %all-to-all-done.1 = bf16[8,584,128]{2,1,0:T(8,128)(2,1)S(1)} async-done(((bf16[8,584,128]{2,1,0:T(8,128)(2,1)}), bf16[8,584,128]{2,1,0:T(8,128)(2,1)S(1)}, u32[]{:S(2)}, u32[]{:S(2)}) %all-to-all-start.1) | async-done | bytes 1196064 | tf_op jit(solution)/shard_map/all_to_all | solution.py:13
  45.7 7.7 %all-to-all-start.2 = ((bf16[16,64,1536]{2,1,0:T(8,128)(2,1)}), bf16[16,64,1536]{2,1,0:T(8,128)(2,1)S(1)}, u32[]{:S(2)}, u32[]{:S(2)}) async-start(bf16[16,64,1536]{2,1,0:T(8,128)(2,1)} %stack.88), calls=%async_computation.2 | async-start | bytes 6291456 | tf_op jit(solution)/shard_map/all_to_all | solution.py:57
  57.1 3.1 reshape.615
  60.2 34.8 %all-to-all-done.2 = bf16[16,64,1536]{2,1,0:T(8,128)(2,1)S(1)} async-done(((bf16[16,64,1536]{2,1,0:T(8,128)(2,1)}), bf16[16,64,1536]{2,1,0:T(8,128)(2,1)S(1)}, u32[]{:S(2)}, u32[]{:S(2)}) %all-to-all-start.2) | async-done | bytes 3145760 | tf_op jit(solution)/shard_map/all_to_all | solution.py:57
  110.0 4.4 all-to-all-start.3
  114.9 16.8 %all-to-all-done.3 = bf16[8,584,128]{2,1,0:T(8,128)(2,1)} async-done(((bf16[8,584,128]{2,1,0:T(8,128)(2,1)}), bf16[8,584,128]{2,1,0:T(8,128)(2,1)}, u32[]{:S(2)}, u32[]{:S(2)}) %all-to-all-start.3) | async-done | bytes 1196064 | tf_op jit(solution)/shard_map/all_to_all | solution.py:48
  133.6 8.7 %all_to_all.152 = f32[8,1,1168]{2,1,0:T(1,128)S(1)} all-to-all(f32[8,1,1168]{2,1,0:T(1,128)S(1)} %broadcast_in_dim.120), channel_id=1, replica_groups=mesh['tok'=16,'wid'=8] {'wid'}, dimensions={0} | all-to-all | bytes 74752 | tf_op jit(solution)/shard_map/all_to_all | solution.py:13
  144.5 4.6 all-to-all-start.5
  149.7 15.8 %all-to-all-done.5 = bf16[8,584,128]{2,1,0:T(8,128)(2,1)} async-done(((bf16[8,584,128]{2,1,0:T(8,128)(2,1)}), bf16[8,584,128]{2,1,0:T(8,128)(2,1)}, u32[]{:S(2)}, u32[]{:S(2)}) %all-to-all-start.5) | async-done | bytes 1196064 | tf_op jit(solution)/shard_map/all_to_all | solution.py:13
  165.4 5.8 fusion.25
  174.7 4.4 all-to-all-start.6
  179.7 14.9 %all-to-all-done.6 = bf16[8,584,128]{2,1,0:T(8,128)(2,1)} async-done(((bf16[8,584,128]{2,1,0:T(8,128)(2,1)}), bf16[8,584,128]{2,1,0:T(8,128)(2,1)}, u32[]{:S(2)}, u32[]{:S(2)}) %all-to-all-start.6) | async-done | bytes 1196064 | tf_op jit(solution)/shard_map/all_to_all | solution.py:48
  197.7 4.0 all-to-all-start.7
  203.2 4.7 all-to-all-done.7
  210.9 10.7 %all-to-all-start.9 = ((bf16[16,64,1536]{2,1,0:T(8,128)(2,1)}), bf16[16,64,1536]{2,1,0:T(8,128)(2,1)}, u32[]{:S(2)}, u32[]{:S(2)}) async-start(bf16[16,64,1536]{2,1,0:T(8,128)(2,1)} %stack.89), calls=%async_computation.9 | async-start | bytes 6291456 | tf_op jit(solution)/shard_map/all_to_all | solution.py:57
  224.3 38.9 %all-to-all-done.9 = bf16[16,64,1536]{2,1,0:T(8,128)(2,1)} async-done(((bf16[16,64,1536]{2,1,0:T(8,128)(2,1)}), bf16[16,64,1536]{2,1,0:T(8,128)(2,1)}, u32[]{:S(2)}, u32[]{:S(2)}) %all-to-all-start.9) | async-done | bytes 3145760 | tf_op jit(solution)/shard_map/all_to_all | solution.py:57
  265.4 4.4 all-to-all-start.8
  274.4 12.7 %all-to-all-done.8 = bf16[8,584,128]{2,1,0:T(8,128)(2,1)} async-done(((bf16[8,584,128]{2,1,0:T(8,128)(2,1)}), bf16[8,584,128]{2,1,0:T(8,128)(2,1)}, u32[]{:S(2)}, u32[]{:S(2)}) %all-to-all-start.8) | async-done | bytes 1196064 | tf_op jit(solution)/shard_map/all_to_all | solution.py:13
  289.7 3.1 reshape.616
  308.7 20.0 %all_to_all.153 = bf16[8,584,128]{2,1,0:T(8,128)(2,1)S(1)} all-to-all(bf16[8,584,128]{2,1,0:T(8,128)(2,1)S(1)} %bitcast.384), channel_id=1, replica_groups=mesh['tok'=16,'wid'=8] {'wid'}, dimensions={0} | all-to-all | bytes 2392064 | tf_op jit(solution)/shard_map/all_to_all | solution.py:48
  330.8 8.7 %all_to_all.154 = f32[8,1,1168]{2,1,0:T(1,128)S(1)} all-to-all(f32[8,1,1168]{2,1,0:T(1,128)S(1)} %broadcast_in_dim.124), channel_id=1, replica_groups=mesh['tok'=16,'wid'=8] {'wid'}, dimensions={0} | all-to-all | bytes 74752 | tf_op jit(solution)/shard_map/all_to_all | solution.py:13
  341.0 18.8 %all_to_all.155 = bf16[8,584,128]{2,1,0:T(8,128)(2,1)} all-to-all(bf16[8,584,128]{2,1,0:T(8,128)(2,1)S(1)} %broadcast_in_dim.125), channel_id=1, replica_groups=mesh['tok'=16,'wid'=8] {'wid'}, dimensions={0} | all-to-all | bytes 2392064 | tf_op jit(solution)/shard_map/all_to_all | solution.py:13
  361.0 4.8 all-to-all-start.14
  365.8 6.0 fusion.28
  371.8 8.2 %all-to-all-done.14 = bf16[8,584,128]{2,1,0:T(8,128)(2,1)} async-done(((bf16[8,584,128]{2,1,0:T(8,128)(2,1)}), bf16[8,584,128]{2,1,0:T(8,128)(2,1)}, u32[]{:S(2)}, u32[]{:S(2)}) %all-to-all-start.14) | async-done | bytes 1196064 | tf_op jit(solution)/shard_map/all_to_all | solution.py:13
  380.0 3.1 convert_reduce_fusion.12
  386.6 4.3 all-to-all-start.15
  394.4 9.8 %all-to-all-done.15 = bf16[8,584,128]{2,1,0:T(8,128)(2,1)} async-done(((bf16[8,584,128]{2,1,0:T(8,128)(2,1)}), bf16[8,584,128]{2,1,0:T(8,128)(2,1)}, u32[]{:S(2)}, u32[]{:S(2)}) %all-to-all-start.15) | async-done | bytes 1196064 | tf_op jit(solution)/shard_map/all_to_all | solution.py:48
  404.2 4.2 all-to-all-start.13
  411.4 10.3 %all-to-all-done.13 = bf16[8,584,128]{2,1,0:T(8,128)(2,1)} async-done(((bf16[8,584,128]{2,1,0:T(8,128)(2,1)}), bf16[8,584,128]{2,1,0:T(8,128)(2,1)}, u32[]{:S(2)}, u32[]{:S(2)}) %all-to-all-start.13) | async-done | bytes 1196064 | tf_op jit(solution)/shard_map/all_to_all | solution.py:48
  422.3 3.3 all-to-all-start.16
  427.9 4.0 all-to-all-done.16
  436.0 4.4 all-to-all-start.17
  440.5 12.3 %all-to-all-done.17 = bf16[8,584,128]{2,1,0:T(8,128)(2,1)} async-done(((bf16[8,584,128]{2,1,0:T(8,128)(2,1)}), bf16[8,584,128]{2,1,0:T(8,128)(2,1)}, u32[]{:S(2)}, u32[]{:S(2)}) %all-to-all-start.17) | async-done | bytes 1196064 | tf_op jit(solution)/shard_map/all_to_all | solution.py:13
  457.0 3.3 convert_reduce_fusion.16
  466.8 15.1 %all_to_all.156 = bf16[8,584,128]{2,1,0:T(8,128)(2,1)S(1)} all-to-all(bf16[8,584,128]{2,1,0:T(8,128)(2,1)S(1)} %bitcast.385), channel_id=1, replica_groups=mesh['tok'=16,'wid'=8] {'wid'}, dimensions={0} | all-to-all | bytes 2392064 | tf_op jit(solution)/shard_map/all_to_all | solution.py:48
  483.6 8.7 %all_to_all.157 = f32[8,1,1168]{2,1,0:T(1,128)S(1)} all-to-all(f32[8,1,1168]{2,1,0:T(1,128)S(1)} %broadcast_in_dim.129), channel_id=1, replica_groups=mesh['tok'=16,'wid'=8] {'wid'}, dimensions={0} | all-to-all | bytes 74752 | tf_op jit(solution)/shard_map/all_to_all | solution.py:13
  496.4 4.2 all-to-all-start.20
  500.7 12.3 %all-to-all-done.20 = bf16[8,584,128]{2,1,0:T(8,128)(2,1)} async-done(((bf16[8,584,128]{2,1,0:T(8,128)(2,1)}), bf16[8,584,128]{2,1,0:T(8,128)(2,1)}, u32[]{:S(2)}, u32[]{:S(2)}) %all-to-all-start.20) | async-done | bytes 1196064 | tf_op jit(solution)/shard_map/all_to_all | solution.py:13
  513.0 3.1 convert_reduce_fusion.13
  519.7 4.6 all-to-all-start.21
  524.3 3.4 convolution_convert_fusion.9
  530.1 3.5 convolution_convert_fusion.8
  538.6 3.7 reshape.613
  542.3 3.3 convolution_convert_fusion.12
  549.6 5.7 all-to-all-start.22
  572.5 5.8 all-to-all-start.23
  578.4 3.1 pad_maximum_fusion.1
  581.7 4.0 reshape.614
  586.1 3.5 convolution_convert_fusion.11
  591.9 3.5 convolution_convert_fusion.10
  600.4 3.7 reshape.608
  625.3 10.3 %all-to-all-start.27 = ((f32[16,1,1536]{2,1,0:T(1,128)}), f32[16,1,1536]{2,1,0:T(1,128)S(1)}, u32[]{:S(2)}, u32[]{:S(2)}) async-start(f32[16,1,1536]{2,1,0:T(1,128)} %broadcast_in_dim.135), calls=%async_computation.27 | async-start | bytes 196608 | tf_op jit(solution)/shard_map/all_to_all | solution.py:13
  638.9 4.5 all-to-all-done.27
  643.4 5.7 all-to-all-start.24
  649.4 19.0 %reduce-scatter.5.cloned.1.call-done = bf16[768,128]{1,0:T(8,128)(2,1)} async-done(((bf16[12288,128]{1,0:T(8,128)(2,1)}), bf16[768,128]{1,0:T(8,128)(2,1)}) %reduce-scatter.5.cloned.1.call-update) | async-done | bytes 196624 | tf_op jit(solution)/shard_map/reduce_scatter | solution.py:75
  673.1 4.3 all-to-all-start.25
  677.5 6.2 all-to-all-done.25
  684.4 5.3 all-to-all-start.26
  691.0 6.6 all-to-all-done.26
  701.1 45.6 %reduce-scatter.3.cloned.1.call-done = bf16[768,128]{1,0:T(8,128)(2,1)} async-done(((bf16[12288,128]{1,0:T(8,128)(2,1)}), bf16[768,128]{1,0:T(8,128)(2,1)}) %reduce-scatter.3.cloned.1.call-update) | async-done | bytes 196624 | tf_op jit(solution)/shard_map/reduce_scatter | solution.py:75
  (395 shorter events, 192.8 us)
Async XLA Ops:
  9.0 11.8 %all-to-all-start = ((f32[8,1,1168]{2,1,0:T(1,128)}), f32[8,1,1168]{2,1,0:T(1,128)S(1)}, u32[]{:S(2)}, u32[]{:S(2)}) async-start(f32[8,1,1168]{2,1,0:T(1,128)} %broadcast_in_dim.60), calls=%async_computation | async-start | bytes 81920 | tf_op jit(solution)/shard_map/all_to_all | solution.py:13
  15.9 7.9 %copy-start.56 = (f32[128]{0:T(128)}, f32[128]{0:T(128)S(1)}, u32[]{:S(2)}) copy-start(f32[128]{0:T(128)S(1)} %get-tuple-element.187) | copy-start | bytes 1540
  15.9 126.6 %copy-start.58 = (f32[128]{0:T(128)}, f32[128]{0:T(128)S(1)}, u32[]{:S(2)}) copy-start(f32[128]{0:T(128)S(1)} %get-tuple-element.188) | copy-start | bytes 1540
  23.8 3.7 copy-start.40
  23.8 4.4 copy-start.51
  23.8 5.1 copy-start.38
  23.8 5.7 copy-start.39
  23.8 19.8 %all-to-all-start.1 = ((bf16[8,584,128]{2,1,0:T(8,128)(2,1)}), bf16[8,584,128]{2,1,0:T(8,128)(2,1)S(1)}, u32[]{:S(2)}, u32[]{:S(2)}) async-start(bf16[8,584,128]{2,1,0:T(8,128)(2,1)} %broadcast_in_dim.61), calls=%async_computation.1 | async-start | bytes 2392064 | tf_op jit(solution)/shard_map/all_to_all | solution.py:13
  45.7 7.7 %copy-start.69 = (f32[2,2,128]{2,1,0:T(2,128)S(1)}, f32[2,2,128]{2,1,0:T(2,128)}, u32[]{:S(2)}) copy-start(f32[2,2,128]{2,1,0:T(2,128)} %param.18) | copy-start | bytes 6148
  45.7 8.5 %copy-start.54 = (s32[584]{0:T(1024)S(1)}, s32[584]{0:T(1024)}, u32[]{:S(2)}) copy-start(s32[584]{0:T(1024)} %param.14) | copy-start | bytes 7012
  45.7 49.3 %all-to-all-start.2 = ((bf16[16,64,1536]{2,1,0:T(8,128)(2,1)}), bf16[16,64,1536]{2,1,0:T(8,128)(2,1)S(1)}, u32[]{:S(2)}, u32[]{:S(2)}) async-start(bf16[16,64,1536]{2,1,0:T(8,128)(2,1)} %stack.88), calls=%async_computation.2 | async-start | bytes 6291456 | tf_op jit(solution)/shard_map/all_to_all | solution.py:57
  54.1 49.5 %copy-start.62 = (f32[2,64]{1,0:T(2,128)}, f32[2,64]{1,0:T(2,128)S(1)}, u32[]{:S(2)}) copy-start(f32[2,64]{1,0:T(2,128)S(1)} %add.219) | copy-start | bytes 1540
  54.2 51.8 %copy-start.71 = (f32[2,64]{1,0:T(2,128)}, f32[2,64]{1,0:T(2,128)S(1)}, u32[]{:S(2)}) copy-start(f32[2,64]{1,0:T(2,128)S(1)} %add.216) | copy-start | bytes 1540
  54.5 49.1 %copy-start.8 = (pred[584,584]{0,1:T(8,128)(4,1)}, pred[584,584]{0,1:T(8,128)(4,1)S(1)}, u32[]{:S(2)}) copy-start(pred[584,584]{0,1:T(8,128)(4,1)S(1)} %broadcast_compare_fusion) | copy-start | bytes 1023172
  95.0 3.6 copy-start.2
  110.0 4.4 copy-start.74
  110.0 21.8 %all-to-all-start.3 = ((bf16[8,584,128]{2,1,0:T(8,128)(2,1)}), bf16[8,584,128]{2,1,0:T(8,128)(2,1)}, u32[]{:S(2)}, u32[]{:S(2)}) async-start(bf16[8,584,128]{2,1,0:T(8,128)(2,1)} %bitcast.383), calls=%async_computation.3 | async-start | bytes 2392064 | tf_op jit(solution)/shard_map/all_to_all | solution.py:48
  114.4 18.8 %copy-start.7 = (bf16[584,128]{1,0:T(8,128)(2,1)S(1)}, bf16[584,128]{1,0:T(8,128)(2,1)}, u32[]{:S(2)}) copy-start(bf16[584,128]{1,0:T(8,128)(2,1)} %param.13) | copy-start | bytes 448516
  144.4 4.6 copy-start.61
  144.5 21.0 %all-to-all-start.5 = ((bf16[8,584,128]{2,1,0:T(8,128)(2,1)}), bf16[8,584,128]{2,1,0:T(8,128)(2,1)}, u32[]{:S(2)}, u32[]{:S(2)}) async-start(bf16[8,584,128]{2,1,0:T(8,128)(2,1)} %broadcast_in_dim.121), calls=%async_computation.5 | async-start | bytes 2392064 | tf_op jit(solution)/shard_map/all_to_all | solution.py:13
  174.7 4.4 copy-start.34
  174.7 4.5 copy-start.75
  174.7 19.9 %all-to-all-start.6 = ((bf16[8,584,128]{2,1,0:T(8,128)(2,1)}), bf16[8,584,128]{2,1,0:T(8,128)(2,1)}, u32[]{:S(2)}, u32[]{:S(2)}) async-start(bf16[8,584,128]{2,1,0:T(8,128)(2,1)} %bitcast.381), calls=%async_computation.6 | async-start | bytes 2392064 | tf_op jit(solution)/shard_map/all_to_all | solution.py:48
  179.7 22.0 %copy-start.33 = (bf16[64,512]{1,0:T(8,128)(2,1)S(1)}, bf16[64,512]{1,0:T(8,128)(2,1)}, u32[]{:S(2)}) copy-start(bf16[64,512]{1,0:T(8,128)(2,1)} %get-tuple-element.114) | copy-start | bytes 196612
  197.7 10.3 %all-to-all-start.7 = ((f32[8,1,1168]{2,1,0:T(1,128)}), f32[8,1,1168]{2,1,0:T(1,128)}, u32[]{:S(2)}, u32[]{:S(2)}) async-start(f32[8,1,1168]{2,1,0:T(1,128)} %broadcast_in_dim.122), calls=%async_computation.7 | async-start | bytes 81920 | tf_op jit(solution)/shard_map/all_to_all | solution.py:13
  210.9 11.6 %copy-start.60 = (f32[128]{0:T(128)S(1)}, f32[128]{0:T(128)}, u32[]{:S(2)}) copy-start(f32[128]{0:T(128)} %get-tuple-element.186) | copy-start | bytes 1540
  210.9 11.6 %copy-start.66 = (f32[128]{0:T(128)S(1)}, f32[128]{0:T(128)}, u32[]{:S(2)}) copy-start(f32[128]{0:T(128)} %get-tuple-element.157) | copy-start | bytes 1540
  210.9 52.3 %all-to-all-start.9 = ((bf16[16,64,1536]{2,1,0:T(8,128)(2,1)}), bf16[16,64,1536]{2,1,0:T(8,128)(2,1)}, u32[]{:S(2)}, u32[]{:S(2)}) async-start(bf16[16,64,1536]{2,1,0:T(8,128)(2,1)} %stack.89), calls=%async_computation.9 | async-start | bytes 6291456 | tf_op jit(solution)/shard_map/all_to_all | solution.py:57
  265.4 4.4 copy-start.80
  265.4 4.5 copy-start.79
  265.4 21.8 %all-to-all-start.8 = ((bf16[8,584,128]{2,1,0:T(8,128)(2,1)}), bf16[8,584,128]{2,1,0:T(8,128)(2,1)}, u32[]{:S(2)}, u32[]{:S(2)}) async-start(bf16[8,584,128]{2,1,0:T(8,128)(2,1)} %broadcast_in_dim.123), calls=%async_computation.8 | async-start | bytes 2392064 | tf_op jit(solution)/shard_map/all_to_all | solution.py:13
  328.8 10.8 %copy-start.55 = (f32[128]{0:T(128)S(1)}, f32[128]{0:T(128)}, u32[]{:S(2)}) copy-start(f32[128]{0:T(128)} %get-tuple-element.189) | copy-start | bytes 1540
  328.8 10.8 %copy-start.65 = (f32[128]{0:T(128)S(1)}, f32[128]{0:T(128)}, u32[]{:S(2)}) copy-start(f32[128]{0:T(128)} %get-tuple-element.154) | copy-start | bytes 1540
  341.0 18.8 %copy-start.32 = (bf16[584,128]{1,0:T(8,128)(2,1)S(1)}, bf16[584,128]{1,0:T(8,128)(2,1)}, u32[]{:S(2)}) copy-start(bf16[584,128]{1,0:T(8,128)(2,1)} %param.25) | copy-start | bytes 448516
  361.0 4.8 copy-start.70
  361.0 19.0 %all-to-all-start.14 = ((bf16[8,584,128]{2,1,0:T(8,128)(2,1)}), bf16[8,584,128]{2,1,0:T(8,128)(2,1)}, u32[]{:S(2)}, u32[]{:S(2)}) async-start(bf16[8,584,128]{2,1,0:T(8,128)(2,1)} %broadcast_in_dim.126), calls=%async_computation.14 | async-start | bytes 2392064 | tf_op jit(solution)/shard_map/all_to_all | solution.py:13
  386.6 17.6 %all-to-all-start.15 = ((bf16[8,584,128]{2,1,0:T(8,128)(2,1)}), bf16[8,584,128]{2,1,0:T(8,128)(2,1)}, u32[]{:S(2)}, u32[]{:S(2)}) async-start(bf16[8,584,128]{2,1,0:T(8,128)(2,1)} %bitcast.382), calls=%async_computation.15 | async-start | bytes 2392064 | tf_op jit(solution)/shard_map/all_to_all | solution.py:48
  404.2 17.5 %all-to-all-start.13 = ((bf16[8,584,128]{2,1,0:T(8,128)(2,1)}), bf16[8,584,128]{2,1,0:T(8,128)(2,1)}, u32[]{:S(2)}, u32[]{:S(2)}) async-start(bf16[8,584,128]{2,1,0:T(8,128)(2,1)} %bitcast.380), calls=%async_computation.13 | async-start | bytes 2392064 | tf_op jit(solution)/shard_map/all_to_all | solution.py:48
  410.6 21.4 %copy-start.64 = (f32[128]{0:T(128)S(1)}, f32[128]{0:T(128)}, u32[]{:S(2)}) copy-start(f32[128]{0:T(128)} %get-tuple-element.158) | copy-start | bytes 1540
  422.3 9.6 %all-to-all-start.16 = ((f32[8,1,1168]{2,1,0:T(1,128)}), f32[8,1,1168]{2,1,0:T(1,128)S(1)}, u32[]{:S(2)}, u32[]{:S(2)}) async-start(f32[8,1,1168]{2,1,0:T(1,128)} %broadcast_in_dim.127), calls=%async_computation.16 | async-start | bytes 81920 | tf_op jit(solution)/shard_map/all_to_all | solution.py:13
  436.0 16.8 %all-to-all-start.17 = ((bf16[8,584,128]{2,1,0:T(8,128)(2,1)}), bf16[8,584,128]{2,1,0:T(8,128)(2,1)}, u32[]{:S(2)}, u32[]{:S(2)}) async-start(bf16[8,584,128]{2,1,0:T(8,128)(2,1)} %broadcast_in_dim.128), calls=%async_computation.17 | async-start | bytes 2392064 | tf_op jit(solution)/shard_map/all_to_all | solution.py:13
  460.2 4.2 copy-start.23
  496.4 16.6 %all-to-all-start.20 = ((bf16[8,584,128]{2,1,0:T(8,128)(2,1)}), bf16[8,584,128]{2,1,0:T(8,128)(2,1)}, u32[]{:S(2)}, u32[]{:S(2)}) async-start(bf16[8,584,128]{2,1,0:T(8,128)(2,1)} %broadcast_in_dim.130), calls=%async_computation.20 | async-start | bytes 2392064 | tf_op jit(solution)/shard_map/all_to_all | solution.py:13
  519.7 4.6 copy-start.50
  519.7 4.6 copy-start.53
  519.7 25.9 %all-to-all-start.21 = ((bf16[8,584,128]{2,1,0:T(8,128)(2,1)}), bf16[8,584,128]{2,1,0:T(8,128)(2,1)}, u32[]{:S(2)}, u32[]{:S(2)}) async-start(bf16[8,584,128]{2,1,0:T(8,128)(2,1)} %bitcast.379), calls=%async_computation.21 | async-start | bytes 2392064 | tf_op jit(solution)/shard_map/all_to_all | solution.py:48
  549.6 19.4 %all-to-all-start.22 = ((f32[8,1,1168]{2,1,0:T(1,128)}), f32[8,1,1168]{2,1,0:T(1,128)S(1)}, u32[]{:S(2)}, u32[]{:S(2)}) async-start(f32[8,1,1168]{2,1,0:T(1,128)} %broadcast_in_dim.131), calls=%async_computation.22 | async-start | bytes 81920 | tf_op jit(solution)/shard_map/all_to_all | solution.py:13
  572.5 5.9 copy-start.22
  572.5 31.6 %all-to-all-start.23 = ((bf16[8,584,128]{2,1,0:T(8,128)(2,1)}), bf16[8,584,128]{2,1,0:T(8,128)(2,1)}, u32[]{:S(2)}, u32[]{:S(2)}) async-start(bf16[8,584,128]{2,1,0:T(8,128)(2,1)} %broadcast_in_dim.132), calls=%async_computation.23 | async-start | bytes 2392064 | tf_op jit(solution)/shard_map/all_to_all | solution.py:13
  578.4 90.0 %reduce-scatter.5.cloned.1.call-start = ((), (), s32[]{:S(2)}) async-start(), calls=%async_computation.31 | async-start | bytes 3342336 | tf_op jit(solution)/shard_map/reduce_scatter | solution.py:75
  585.8 160.9 %reduce-scatter.3.cloned.1.call-start = ((), (), s32[]{:S(2)}) async-start(), calls=%async_computation.30 | async-start | bytes 3342336 | tf_op jit(solution)/shard_map/reduce_scatter | solution.py:75
  611.7 4.4 copy-start.27
  623.9 11.7 %copy-start.26 = (bf16[2,64,584]{2,1,0:T(8,128)(2,1)S(1)}, bf16[2,64,584]{2,1,0:T(8,128)(2,1)}, u32[]{:S(2)}) copy-start(bf16[2,64,584]{2,1,0:T(8,128)(2,1)} %get-tuple-element.181) | copy-start | bytes 448516
  623.9 11.7 %copy-start.28 = (bf16[2,64,584]{2,1,0:T(8,128)(2,1)S(1)}, bf16[2,64,584]{2,1,0:T(8,128)(2,1)}, u32[]{:S(2)}) copy-start(bf16[2,64,584]{2,1,0:T(8,128)(2,1)} %copy-done.27) | copy-start | bytes 448516
  623.9 11.7 %copy-start.31 = (bf16[2,64,584]{2,1,0:T(8,128)(2,1)S(1)}, bf16[2,64,584]{2,1,0:T(8,128)(2,1)}, u32[]{:S(2)}) copy-start(bf16[2,64,584]{2,1,0:T(8,128)(2,1)} %copy-done.30) | copy-start | bytes 448516
  625.3 18.1 %all-to-all-start.27 = ((f32[16,1,1536]{2,1,0:T(1,128)}), f32[16,1,1536]{2,1,0:T(1,128)S(1)}, u32[]{:S(2)}, u32[]{:S(2)}) async-start(f32[16,1,1536]{2,1,0:T(1,128)} %broadcast_in_dim.135), calls=%async_computation.27 | async-start | bytes 196608 | tf_op jit(solution)/shard_map/all_to_all | solution.py:13
  643.4 27.7 %all-to-all-start.24 = ((bf16[8,584,128]{2,1,0:T(8,128)(2,1)}), bf16[8,584,128]{2,1,0:T(8,128)(2,1)S(1)}, u32[]{:S(2)}, u32[]{:S(2)}) async-start(bf16[8,584,128]{2,1,0:T(8,128)(2,1)} %bitcast.353), calls=%async_computation.24 | async-start | bytes 2392064 | tf_op jit(solution)/shard_map/all_to_all | solution.py:48
  649.2 22.7 %copy-start.42 = (f32[584]{0:T(1024)S(1)}, f32[584]{0:T(1024)}, u32[]{:S(2)}) copy-start(f32[584]{0:T(1024)} %copy-done.41) | copy-start | bytes 7012
  649.2 22.7 %copy-start.44 = (f32[584]{0:T(1024)S(1)}, f32[584]{0:T(1024)}, u32[]{:S(2)}) copy-start(f32[584]{0:T(1024)} %copy-done.43) | copy-start | bytes 7012
  649.3 22.7 %copy-start.57 = (f32[128]{0:T(128)S(1)}, f32[128]{0:T(128)}, u32[]{:S(2)}) copy-start(f32[128]{0:T(128)} %copy-done.56) | copy-start | bytes 1540
  670.9 6.5 copy-start.78
  671.1 18.7 %copy-start.21 = (f32[584,128]{1,0:T(8,128)S(1)}, f32[584,128]{1,0:T(8,128)}, u32[]{:S(2)}) copy-start(f32[584,128]{1,0:T(8,128)} %get-tuple-element.97) | copy-start | bytes 897028
  673.1 10.6 %all-to-all-start.25 = ((f32[8,1,1168]{2,1,0:T(1,128)}), f32[8,1,1168]{2,1,0:T(1,128)S(1)}, u32[]{:S(2)}, u32[]{:S(2)}) async-start(f32[8,1,1168]{2,1,0:T(1,128)} %broadcast_in_dim.133), calls=%async_computation.25 | async-start | bytes 81920 | tf_op jit(solution)/shard_map/all_to_all | solution.py:13
  684.4 13.2 %all-to-all-start.26 = ((f32[16,1,1536]{2,1,0:T(1,128)}), f32[16,1,1536]{2,1,0:T(1,128)S(1)}, u32[]{:S(2)}, u32[]{:S(2)}) async-start(f32[16,1,1536]{2,1,0:T(1,128)} %broadcast_in_dim.134), calls=%async_computation.26 | async-start | bytes 196608 | tf_op jit(solution)/shard_map/all_to_all | solution.py:13
  (44 other events, 67.0 us)
Sparse Core Ops, SparseCore 0:
  585.9 82.4 reduce-scatter.4
  672.5 74.1 reduce-scatter.2
